TPU v7x, 1024 devices: a whole 4x8x16 slice. The times are simulated.
1024 devices in a mesh: band: 32 (over y, x), set: 32 (over z, core).
Axes of the slice: x: 4, y: 8, z: 16, core: 2. Of those that a mesh axis runs over, the one named last changes fastest.
Arguments:
- grid: float32 [64, 5152, 128], P('band', 'set'), may hold values from -6 to 6
- row_points: int32 [64], P('band'), may hold values from 20 to 5136, as said below
- legendre: bfloat16 [640, 64, 1408], P('set'), may hold values from -0.5 to 0.5
Outputs:
- spectra: float32 [640, 1408, 128], P('set', 'band')
Inputs may be any that keep to these rules, and one draw needn't show every extreme that they name: row_points[r] is 4 j + 20 for some row j of the model grid with r * (20) <= j < (r + 1) * 20; the last row has 5136 points.
All inputs are finite; a program needn't handle non-finite values.
Results may differ from a plain program's by a relative error of at most 0.0029.
Values may be sent and summed in bfloat16 or wider, within the bound.
A program may use at most 32 MiB of HBM per device.

v0:
```python
import math

import jax
import jax.numpy as jnp
from jax import lax
from jax.sharding import PartitionSpec as P

TRUNC = 1279


def selection(pair_ids, slot_ids):
    is_first = slot_ids[None, :] <= TRUNC - pair_ids[:, None]
    parity = jnp.where(
        is_first, slot_ids[None, :] % 2, (slot_ids[None, :] - 1 - TRUNC + pair_ids[:, None]) % 2
    )
    selector = jnp.where(is_first, 0, 2) + parity
    class_ids = jnp.arange(4, dtype=jnp.int32)
    return (selector[:, :, None] == class_ids[None, None, :]).astype(jnp.float32)


def wave_numbers(position, pair_count):
    within = position % (2 * pair_count)
    owned_pair = position // (2 * pair_count) * pair_count + within % pair_count
    return jnp.where(within < pair_count, owned_pair, TRUNC - owned_pair)


def shards(grid, row_points, legendre):
    set_index = lax.axis_index("set")
    band_index = lax.axis_index("band")
    band_size = lax.axis_size("band")
    row_count, point_count, flat_width = grid.shape
    columns = flat_width // 2
    pair_count = legendre.shape[0]
    slot_count = legendre.shape[2] // band_size
    length_float = row_points.astype(jnp.float32)
    row_scale = lax.rsqrt(length_float)
    point_ids = set_index * point_count + jnp.arange(point_count, dtype=jnp.int32)
    in_row = point_ids[None, :] < row_points[:, None]
    grid_split = grid.reshape(row_count, point_count, 2, columns)
    position = jnp.arange(2 * pair_count * lax.axis_size("set"), dtype=jnp.int32)
    wave_ids = wave_numbers(position, pair_count)
    residue = point_ids[None, :, None] * wave_ids[None, None, :] % row_points[:, None, None]
    phases = residue.astype(jnp.float32) * (2.0 * math.pi / length_float)[:, None, None]
    usable = in_row[:, :, None] & (wave_ids[None, None, :] <= (row_points[:, None, None] - 1) // 2)
    cosine_part = jnp.where(usable, jnp.cos(phases) * row_scale[:, None, None], 0.0)
    sine_part = jnp.where(usable, -jnp.sin(phases) * row_scale[:, None, None], 0.0)
    table = jnp.stack([cosine_part, sine_part], axis=2)
    fourier = jnp.einsum("rqhc,rqem->mhrec", grid_split, table, precision=lax.Precision.HIGHEST)
    halves = jnp.stack([fourier[:, 0] + fourier[:, 1], fourier[:, 0] - fourier[:, 1]], axis=1)
    sums = lax.psum_scatter(
        halves.reshape(2 * pair_count * lax.axis_size("set"), 2, row_count, 2 * columns),
        "set",
        scatter_dimension=0,
        tiled=True,
    )
    rounded = sums.astype(jnp.bfloat16)
    sources = rounded.reshape(2, pair_count, 2, row_count, 2 * columns).transpose(1, 0, 2, 3, 4)
    sources = sources.reshape(pair_count, 4, row_count, 2 * columns)
    pair_ids = set_index * pair_count + jnp.arange(pair_count, dtype=jnp.int32)
    slot_ids = band_index * slot_count + jnp.arange(slot_count, dtype=jnp.int32)
    weights = selection(pair_ids, slot_ids)
    legend_mine = lax.dynamic_slice_in_dim(legendre, band_index * slot_count, slot_count, 2)
    products = jnp.einsum(
        "prk,pjrc->pkjc",
        legend_mine,
        lax.all_gather(sources, "band", axis=2, tiled=True),
        preferred_element_type=jnp.float32,
    )
    return jnp.sum(products * weights[:, :, :, None], axis=2)


def solution(mesh):
    return jax.shard_map(
        shards,
        mesh=mesh,
        in_specs=(P("band", "set", None), P("band"), P("set", None, None)),
        out_specs=P("set", "band", None),
        check_vma=False,
    )
```

profile of v0, /device:TPU:56, one launch (start us, length us, event | category | flops | bytes accessed | tf_op | source)
XLA Modules:
  0.0 269.3 jit_solution(13733127831934488392)
XLA Ops:
  6.5 0.0 all-gather.2.cloned.1.call-start
  6.6 0.7 and_select_fusion.3
  7.2 0.7 convert_divide_fusion
  7.9 0.7 broadcast_compare_fusion.2
  8.6 0.7 broadcast_compare_fusion.1
  9.3 0.1 broadcast_multiply_fusion
  9.4 0.1 broadcast_compare_fusion
  9.5 1.0 copy.18
  10.5 23.3 %and_select_fusion.1 = (f32[2,161,1,1280]{3,1,2,0:T(8,128)S(1)}, f32[2,161,1,1280]{3,1,2,0:T(8,128)S(1)}) fusion(f32[2]{0:T(128)S(1)} %get-tuple-element.12, f32[2]{0:T(128)S(1)} %get-tuple-element.11, s32[2]{0:T(128)S(1)} %get-tuple-element.10, s32[161,1280]{1,0:T(8,128)S(1)} %broadcast_multiply_fusion, pred[2]{0:T(512)(128)(4,1)S(1)} %broadcast_compare_fusion.2, ...), kind=kLoop, calls=%fused_computation.11 | loop fusion | flops 6182400 | bytes 4124508 | tf_op jit(solution)/shard_map/jit(_where)/select_n | solution.py:45
  33.9 3.0 %fusion.3 = f32[1280,2,2,2,64]{0,4,1,3,2:T(8,128)S(1)} fusion(f32[2,161,2,64,1]{1,3,2,4,0:T(8,128)S(1)} %bitcast.30, f32[2,161,1,1280]{3,1,2,0:T(8,128)S(1)} %get-tuple-element.8, f32[2,161,1,1280]{3,1,2,0:T(8,128)S(1)} %get-tuple-element.7), kind=kOutput, calls=%fused_computation.8 | convolution fusion | flops 1266979840 | bytes 6083584 | tf_op jit(solution)/shard_map/rqhc,rqem->mhrec/dot_general | solution.py:48
  36.8 0.2 slice_add_fusion
  37.1 2.1 copy.19
  39.1 2.0 copy.20
  41.1 2.5 pad_maximum_fusion
  43.7 128.5 %all-reduce.2 = bf16[1280,2,2,128]{3,2,1,0:T(2,128)(2,1)} all-reduce(f32[1280,2,2,128]{3,2,1,0:T(2,128)S(1)} %pad_maximum_fusion), channel_id=2, replica_groups=mesh['band'=32,'set'=32] {'set'}, use_global_device_ids=true, to_apply=%region_0.1.clone | all-reduce | flops 655360 | bytes 3932160
  172.1 1.3 dynamic-slice
  174.1 0.8 dynamic-slice_convert_fusion
  174.9 0.6 copy.22
  175.5 0.0 all-gather.2.cloned.1.call-update
  175.6 0.1 fusion.21
  175.7 83.2 %all-gather.2.cloned.1.call-done = bf16[20,4,64,128]{3,1,0,2:T(4,128)(2,1)} async-done(((bf16[20,4,2,128]{3,1,0,2:T(4,128)(2,1)}), bf16[20,4,64,128]{3,1,0,2:T(4,128)(2,1)}) %all-gather.2.cloned.1.call-update) | async-done | bytes 1310736 | tf_op jit(solution)/shard_map/all_gather | solution.py:66
  258.9 3.5 %multiply_reduce_fusion = f32[20,44,128]{2,1,0:T(8,128)} fusion(bf16[20,4,64,128]{3,1,0,2:T(4,128)(2,1)} %all-gather.2.cloned.1.call-done, f32[20,44,4]{1,2,0:T(4,128)S(1)} %fusion.16, bf16[20,64,1408]{2,1,0:T(8,128)(2,1)} %param.5, s32[]{:T(128)S(6)} %select_n.130), kind=kOutput, calls=%fused_computation.12 | convolution fusion | flops 58460160 | bytes 2103044 | tf_op jit(solution)/shard_map/prk,pjrc->pkjc/dot_general | solution.py:63
  (7 shorter events, 0.1 us)
Async XLA Ops:
  6.5 252.4 %all-gather.2.cloned.1.call-start = ((), (), s32[]{:S(2)}) async-start(), calls=%async_computation | async-start | bytes 1351680 | tf_op jit(solution)/shard_map/all_gather | solution.py:66
Sparse Core Ops, SparseCore 0:
  175.7 83.2 all-gather.1
where the time goes:
time: 271 us; the launch traced here: 269 us
  blocking collectives  128 us (47%)
  waiting for transfers between devices  83.2 us (31%)
  other arithmetic  29.1 us (11%)
  between operations  14.1 us (5%)
  local copies, waits for them, and re-layouts  7.87 us (3%)
  matrix products  6.45 us (2%)
    unnamed x1, blocking collectives  128 us
    all_gather x1, waiting for transfers between devices, shards(): lax.all_gather(sources, 'band', axis=2, tiled=True)  83.2 us
    select_n x1, other arithmetic, shards(): jnp.where(usable, jnp.cos(phases) * row_scale[:, None, None], 0.0)  23.3 us
  transfers between devices with their start and end apart: 1, of which 1 were waited for; matrix products, arithmetic and copies ran while one was open for 0% of the time, Pallas kernels for 0%

commit v1 on v0

v1 whole, which is shorter than its diff:
```python
import functools
import math

import jax
import jax.numpy as jnp
from jax import lax
from jax.experimental import pallas as pl
from jax.experimental.pallas import tpu as pltpu
from jax.sharding import PartitionSpec as P

MESH = pl.DeviceIdType.MESH
CHIPS_X = 4
WINDOW = 256
SIN_TERMS = (1.0, -1 / 6, 1 / 120, -1 / 5040, 1 / 362880, -1 / 39916800)
COS_TERMS = (1.0, -1 / 2, 1 / 24, -1 / 720, 1 / 40320, -1 / 3628800, 1 / 479001600)


def horner(terms, square):
    total = jnp.full_like(square, terms[-1])
    for term in terms[-2::-1]:
        total = total * square + term
    return total


def cos_sin(waves, points, length):
    product = waves * points
    residue = product - jnp.floor(product * (1.0 / length) + 0.5) * length
    half = residue * (math.pi / length)
    square = half * half
    sine = half * horner(SIN_TERMS, square)
    cosine = horner(COS_TERMS, square)
    return 1.0 - 2.0 * sine * sine, 2.0 * sine * cosine


def split(value):
    high = value.astype(jnp.bfloat16)
    return high, (value - high.astype(jnp.float32)).astype(jnp.bfloat16)


def kernel(
    sizes,
    rows_ref,
    grid_ref,
    leg_ref,
    out_ref,
    twin,
    folded,
    grid_high,
    grid_low,
    window,
    leg_rows,
    weights,
    send_r,
    recv_r,
    send_l,
    recv_l,
    packed,
    blocks,
    spread,
    leg_sem,
    twin_sem,
    ring_send,
    ring_recv,
    y_send,
    y_recv,
    x_send,
    x_recv,
):
    bands, sets, nx, pairs, slots, per_device = sizes
    ny, nz = bands // nx, sets // 2
    half = nz // 2
    trunc = 2 * pairs * sets - 1
    group_rows = 2 * pairs
    band, group = lax.axis_index("band"), lax.axis_index("set")
    y, x = lax.div(band, nx), lax.rem(band, nx)
    z, core = lax.div(group, 2), lax.rem(group, 2)
    sibling = z * 2 + 1 - core

    def at_z(position):
        return lax.rem(position + nz, nz) * 2 + core

    right, left = at_z(z + 1), at_z(z - 1)

    def at_y(position):
        return lax.rem(position + ny, ny) * nx + x

    def at_x(position):
        return y * nx + lax.rem(position, nx)

    def needs(side, of_band):
        if side == 0:
            return slots * of_band <= trunc - pairs * group
        return slots * of_band + slots - 1 >= trunc + 1 - (pairs * group + pairs - 1)

    def row_needs(side, of_y):
        return needs(side, of_y * nx + (0 if side == 0 else nx - 1))

    peers = [(band, sibling), (band, right), (band, left)]
    if nz == 2:
        peers.pop()
    peers += [(at_y(y + d), group) for d in range(1, ny)]
    peers += [(at_x(x + d), group) for d in range(1, nx)]
    barrier = pltpu.get_barrier_semaphore()
    for peer in peers:
        pl.semaphore_signal(barrier, inc=1, device_id=peer, device_id_type=MESH)

    first = slots * band
    start = jnp.minimum(lax.div(first, 128) * 128, leg_ref.shape[2] - WINDOW)
    leg_copy = pltpu.make_async_copy(
        leg_ref.at[:, :, pl.ds(pl.multiple_of(start, 128), WINDOW)], window, leg_sem
    )
    leg_copy.start()

    lengths = [rows_ref[q].astype(jnp.float32) for q in range(2)]
    bases = [group * per_device, sibling * per_device]

    def prepare(source, half_index):
        for q in range(2):
            folded[q, 0:per_device, :] = source[pl.ds(q, per_device, stride=2), :]
        for q in range(2):
            value = folded[q]
            point = bases[half_index] + lax.broadcasted_iota(jnp.int32, value.shape, 0)
            lane = lax.broadcasted_iota(jnp.int32, value.shape, 1)
            other = pltpu.roll(value, 64, 1)
            value = jnp.where(lane < 64, value + other, other - value)
            value = value * lax.rsqrt(jnp.full(value.shape, lengths[q], jnp.float32))
            row = lax.broadcasted_iota(jnp.int32, value.shape, 0)
            value = jnp.where((point < rows_ref[q]) & (row < per_device), value, 0.0)
            grid_high[q, half_index], grid_low[q, half_index] = split(value)

    def partials(owners):
        count = len(owners) * group_rows
        index = lax.broadcasted_iota(jnp.int32, (count, 1), 0)
        waves = jnp.zeros((count, 1), jnp.int32)
        for position, owner in enumerate(owners):
            inside = index - position * group_rows
            here = jnp.where(
                inside < pairs, pairs * owner + inside, trunc - pairs * owner - (inside - pairs)
            )
            waves = jnp.where(inside >= 0, here, waves)
        waves = waves.astype(jnp.float32)
        lane = lax.broadcasted_iota(jnp.int32, (1, 256), 1)
        results = []
        for q in range(2):
            length = jnp.full((1, 256), lengths[q], jnp.float32)
            total = jnp.zeros((2 * count, 128), jnp.float32)
            for half_index in range(2):
                points = (bases[half_index] + lane).astype(jnp.float32)
                table = jnp.concatenate(cos_sin(waves, points, length), axis=0)
                high, low = split(table)
                for factor, values in ((high, grid_high), (low, grid_high), (high, grid_low)):
                    total = total + jnp.dot(
                        factor, values[q, half_index], preferred_element_type=jnp.float32
                    )
            results.append(total)
        return results

    def ring_copy(to_right, slot, q):
        side = 0 if to_right else 1
        source, target = (send_r, recv_r) if to_right else (send_l, recv_l)
        return pltpu.make_async_remote_copy(
            src_ref=source.at[slot, q],
            dst_ref=target.at[slot, q],
            send_sem=ring_send.at[side, slot, q],
            recv_sem=ring_recv.at[side, slot, q],
            device_id=(band, right if to_right else left),
            device_id_type=MESH,
        )

    def weights_of(pair):
        values = window[pair].astype(jnp.float32)
        values = pltpu.roll(values, lax.rem(WINDOW - (first - start), WINDOW), 1)[:, :128]
        leg_rows[...] = values
        rows = jnp.concatenate([leg_rows[pl.ds(q, bands, stride=2), :] for q in range(2)], axis=0)
        turned = jnp.transpose(rows)[: weights.shape[2]]
        turned = jnp.concatenate([turned, turned], axis=1)
        slot = first + lax.broadcasted_iota(jnp.int32, turned.shape, 0)
        parity = lax.div(lax.broadcasted_iota(jnp.int32, turned.shape, 1), 2 * bands)
        number = pairs * group + pair
        is_first = slot <= trunc - number
        even = (slot & 1) == parity
        other = ((slot - 1 - trunc + number) & 1) == parity
        weights[0, pair] = jnp.where(is_first & even, turned, 0.0).astype(jnp.bfloat16)
        weights[1, pair] = jnp.where((~is_first) & other, turned, 0.0).astype(jnp.bfloat16)

    folded[:, per_device:, :] = jnp.zeros_like(folded[:, per_device:, :])
    recv_r[0, 0] = jnp.zeros_like(recv_r[0, 0])
    recv_l[0, 1] = jnp.zeros_like(recv_l[0, 1])
    prepare(grid_ref, 0)

    pl.semaphore_wait(barrier, len(peers))
    swap = pltpu.make_async_remote_copy(
        src_ref=grid_ref,
        dst_ref=twin,
        send_sem=twin_sem.at[0],
        recv_sem=twin_sem.at[1],
        device_id=(band, sibling),
        device_id_type=MESH,
    )
    swap.start()
    swap.wait()
    prepare(twin, 1)

    far = partials([at_z(z + half)])
    send_l[0, 0] = far[0]
    ring_copy(False, 0, 0).start()
    send_r[0, 1] = far[1]
    ring_copy(True, 0, 1).start()
    leg_copy.wait()
    per_step = -(-pairs // max(half - 1, 1))

    def weights_step(step):
        def one(index, carry):
            pair = (step - 1) * per_step + index

            @pl.when(pair < pairs)
            def _():
                weights_of(pair)

            return carry

        lax.fori_loop(0, per_step, one, 0)

    def ring_step(step, carry):
        mine = partials([at_z(z + half - step), at_z(z - half + step)])
        for q in range(2):
            for to_right in (True, False):
                source, came = (send_r, recv_r) if to_right else (send_l, recv_l)

                @pl.when((step > 1) | (q == (1 if to_right else 0)))
                def _():
                    ring_copy(to_right, step - 1, q).wait_recv()

                offset = 0 if to_right else group_rows
                for part in range(2):
                    low = 2 * part * group_rows + offset
                    span = slice(part * group_rows, (part + 1) * group_rows)
                    source[step, q, span] = (
                        came[step - 1, q, span] + mine[q][low : low + group_rows]
                    )
                ring_copy(to_right, step, q).start()
        weights_step(step)
        return carry

    lax.fori_loop(1, half, ring_step, 0)
    if half == 1:
        weights_step(1)

    own = partials([group])
    last = half - 1
    for q in range(2):
        for to_right in (True, False):
            if half > 1 or q == (1 if to_right else 0):
                ring_copy(to_right, last, q).wait_recv()

    for q in range(2):
        total = own[q] + recv_r[last, q] + recv_l[last, q]
        index = lax.broadcasted_iota(jnp.int32, (group_rows, 128), 0)
        wave = jnp.where(index < pairs, pairs * group + index, trunc - pairs * group - (index - pairs))
        usable = wave <= lax.div(rows_ref[q] - 1, 2)
        cosine = jnp.where(usable, total[:group_rows], 0.0)
        sine = jnp.where(usable, -total[group_rows:], 0.0)
        lane = lax.broadcasted_iota(jnp.int32, (group_rows, 128), 1)
        parts = (
            jnp.where(lane < 64, cosine, pltpu.roll(sine, 64, 1)),
            jnp.where(lane < 64, pltpu.roll(cosine, 64, 1), sine),
        )
        for parity in range(2):
            for side in range(2):
                at = (parity * 2 + q) * pairs
                packed[side, at : at + pairs] = parts[parity][side * pairs : (side + 1) * pairs]
    for side in range(2):
        blocks[side, band] = packed[side].astype(jnp.bfloat16)

    def y_copy(side, distance):
        return pltpu.make_async_remote_copy(
            src_ref=blocks.at[side, band],
            dst_ref=blocks.at[side, band],
            send_sem=y_send.at[side, distance],
            recv_sem=y_recv.at[side, y],
            device_id=(at_y(y + distance), group),
            device_id_type=MESH,
        )

    def y_arrival(side, source_y):
        spot = blocks.at[side, source_y * nx + x]
        return pltpu.make_async_remote_copy(
            src_ref=spot,
            dst_ref=spot,
            send_sem=y_send.at[side, 0],
            recv_sem=y_recv.at[side, source_y],
            device_id=(at_y(y + 1), group),
            device_id_type=MESH,
        )

    def x_copy(side, source_y, distance):
        spot = blocks.at[side, source_y * nx + x]
        return pltpu.make_async_remote_copy(
            src_ref=spot,
            dst_ref=spot,
            send_sem=x_send.at[side, source_y, distance],
            recv_sem=x_recv.at[side, source_y * nx + x],
            device_id=(at_x(x + distance), group),
            device_id_type=MESH,
        )

    def x_arrival(side, source):
        spot = blocks.at[side, source]
        return pltpu.make_async_remote_copy(
            src_ref=spot,
            dst_ref=spot,
            send_sem=x_send.at[side, 0, 0],
            recv_sem=x_recv.at[side, source],
            device_id=(at_x(x + 1), group),
            device_id_type=MESH,
        )

    def in_turn(index):
        step = lax.div(index + 1, 2)
        return jnp.where(lax.rem(index, 2) == 1, step, ny - step)

    def y_start(index, carry):
        distance = lax.rem(in_turn(index), ny)
        for side in range(2):
            @pl.when(row_needs(side, lax.rem(y + distance, ny)))
            def _():
                y_copy(side, distance).start()

        return carry

    lax.fori_loop(1, ny, y_start, 0)

    def unpack(side, source):
        span = 4 * pairs
        spread[side, pl.ds(pl.multiple_of(source * span, 8), span), :] = blocks[
            side, source
        ].astype(jnp.float32)

    def forward(index, carry):
        source_y = lax.rem(y + in_turn(index), ny)
        for side in range(2):
            @pl.when(row_needs(side, y) & (index > 0))
            def _():
                y_arrival(side, source_y).wait_recv()

            for distance in range(1, nx):
                @pl.when(needs(side, at_x(x + distance)))
                def _():
                    x_copy(side, source_y, distance).start()

            @pl.when(needs(side, band))
            def _():
                unpack(side, source_y * nx + x)

        return carry

    lax.fori_loop(0, ny, forward, 0)

    def collect(index, carry):
        source_y = lax.rem(y + in_turn(index), ny)
        for side in range(2):
            for distance in range(1, nx):
                @pl.when(needs(side, band))
                def _():
                    source = source_y * nx + lax.rem(x + distance, nx)
                    x_arrival(side, source).wait_recv()
                    unpack(side, source)

        return carry

    lax.fori_loop(0, ny, collect, 0)

    def legendre(side, add):
        def one(pair, carry):
            parts = [
                spread[side, pl.ds((2 * parity + q) * pairs + pair, bands, stride=4 * pairs), :]
                for parity in range(2)
                for q in range(2)
            ]
            values = jnp.concatenate(parts, axis=0).astype(jnp.bfloat16)
            result = jnp.dot(weights[side, pair], values, preferred_element_type=jnp.float32)
            result = result[:slots]
            out_ref[pair] = out_ref[pair] + result if add else result
            return carry

        lax.fori_loop(0, pairs, one, 0)

    pl.when(needs(0, band))(lambda: legendre(0, False))
    pl.when(needs(1, band) & ~needs(0, band))(lambda: legendre(1, False))
    pl.when(needs(1, band) & needs(0, band))(lambda: legendre(1, True))

    for to_right in (True, False):
        for q in range(2):
            if q == (1 if to_right else 0):
                ring_copy(to_right, 0, q).wait_send()

    def ring_sent(step, carry):
        for to_right in (True, False):
            for q in range(2):
                ring_copy(to_right, step, q).wait_send()
        return carry

    lax.fori_loop(1, half, ring_sent, 0)

    def y_sent(distance, carry):
        for side in range(2):
            @pl.when(row_needs(side, lax.rem(y + distance, ny)))
            def _():
                y_copy(side, distance).wait_send()

        return carry

    lax.fori_loop(1, ny, y_sent, 0)

    def x_sent(source_y, carry):
        for side in range(2):
            for distance in range(1, nx):
                @pl.when(needs(side, at_x(x + distance)))
                def _():
                    x_copy(side, source_y, distance).wait_send()

        return carry

    lax.fori_loop(0, ny, x_sent, 0)


def shards(nx, grid, row_points, legendre):
    bands, sets = lax.axis_size("band"), lax.axis_size("set")
    pairs, rows, width = legendre.shape
    slots = width // bands
    per_device = grid.shape[1]
    points = jnp.transpose(grid, (1, 0, 2)).reshape(2 * per_device, 128)
    half = sets // 4
    padded = -(-slots // 16) * 16
    group_rows = 2 * pairs
    f32, bf16 = jnp.float32, jnp.bfloat16
    ring = pltpu.VMEM((half, 2, 2 * group_rows, 128), f32)
    return pl.pallas_call(
        functools.partial(kernel, (bands, sets, nx, pairs, slots, per_device)),
        out_shape=jax.ShapeDtypeStruct((pairs, slots, 128), f32),
        in_specs=[
            pl.BlockSpec(memory_space=pltpu.SMEM),
            pl.BlockSpec(memory_space=pltpu.VMEM),
            pl.BlockSpec(memory_space=pl.ANY),
        ],
        out_specs=pl.BlockSpec(memory_space=pltpu.VMEM),
        scratch_shapes=[
            pltpu.VMEM((2 * per_device, 128), f32),
            pltpu.VMEM((2, 256, 128), f32),
            pltpu.VMEM((2, 2, 256, 128), bf16),
            pltpu.VMEM((2, 2, 256, 128), bf16),
            pltpu.VMEM((pairs, rows, WINDOW), bf16),
            pltpu.VMEM((rows, 128), f32),
            pltpu.VMEM((2, pairs, padded, 2 * rows), bf16),
            ring,
            ring,
            ring,
            ring,
            pltpu.VMEM((2, 4 * pairs, 128), f32),
            pltpu.VMEM((2, bands, 4 * pairs, 128), bf16),
            pltpu.VMEM((2, bands * 4 * pairs, 128), f32),
            pltpu.SemaphoreType.DMA,
            pltpu.SemaphoreType.DMA((2,)),
            pltpu.SemaphoreType.DMA((2, half, 2)),
            pltpu.SemaphoreType.DMA((2, half, 2)),
            pltpu.SemaphoreType.DMA((2, bands // nx)),
            pltpu.SemaphoreType.DMA((2, bands // nx)),
            pltpu.SemaphoreType.DMA((2, bands // nx, nx)),
            pltpu.SemaphoreType.DMA((2, bands)),
        ],
        compiler_params=pltpu.CompilerParams(
            collective_id=0, has_side_effects=True, vmem_limit_bytes=40 * 1024 * 1024
        ),
    )(row_points, points, legendre)


def solution(mesh, nx=CHIPS_X):
    return jax.shard_map(
        functools.partial(shards, nx),
        mesh=mesh,
        in_specs=(P("band", "set", None), P("band"), P("set", None, None)),
        out_specs=P("set", "band", None),
        check_vma=False,
    )
```

time: 271 us -> 75.7 us (0.28)
  blocking collectives: 128 us -> 0 us
  waiting for transfers between devices: 83.2 us -> 0 us
  Pallas kernels: 0 us -> 71 us
  other arithmetic: 29.1 us -> 0 us
  between operations: 14.1 us -> 0.02 us
  matrix products: 6.45 us -> 0 us
  local copies, waits for them, and re-layouts: 7.87 us -> 4.48 us
    unnamed x1 -> x0, blocking collectives: 128 us -> none
    all_gather x1 -> x0, waiting for transfers between devices: 83.2 us -> none  [shards(): lax.all_gather(sources, 'band', axis=2, tiled=True)]
    pallas_call x0 -> x1, Pallas kernels: none -> 71 us  [shards(): pl.pallas_call(functools.partial(kernel, (bands, sets, nx, pairs, slots,...]
    select_n x4 -> x0, other arithmetic: 24 us -> none  [the longest x1 23.3 us: shards(): jnp.where(usable, jnp.cos(phases) * row_scale[:, None, None], 0.0)]
    dot_general x2 -> x0, matrix products: 6.45 us -> none  [the longest x1 3.48 us: shards(): jnp.einsum('prk,pjrc->pkjc', legend_mine, lax.all_gather(sources, 'band',...]
    another operation x2 -> x0, local copies, waits for them, and re-layouts: 4.08 us -> none  [shards(): jnp.stack([fourier[:, 0] + fourier[:, 1], fourier[:, 0] - fourier[:, 1]],...]
  transfers between devices with their start and end apart: 1 -> 0, of which waited for: 1 -> 0; matrix products, arithmetic and copies ran while one was open for 0% -> 0% of each run, Pallas kernels for 0% -> 0%
where the time goes in v1:
time: 75.7 us; the launch traced here: 75.5 us
  Pallas kernels  71 us (94%)
  local copies, waits for them, and re-layouts  4.48 us (6%)
    pallas_call x1, Pallas kernels, shards(): pl.pallas_call(functools.partial(kernel, (bands, sets, nx, pairs, slots,...  71 us
    unnamed x5, local copies, waits for them, and re-layouts  3.45 us

profile of v1, /device:TPU:56, one launch (start us, length us, event | category | flops | bytes accessed | tf_op | source)
XLA Modules:
  0.0 75.5 jit_solution(16746882763792234815)
XLA Ops:
  0.0 1.0 %reshape.3.grid_ref = f32[322,128]{1,0:T(8,128)S(1)} reshape(f32[161,2,128]{2,1,0:T(2,128)} %bitcast.1) | data formatting | bytes 329728 | tf_op jit(solution)/shard_map/reshape | solution.py:432
  1.0 0.0 copy-start
  1.0 2.0 %copy-done = bf16[20,64,1408]{2,1,0:T(8,128)(2,1)S(1)} copy-done((bf16[20,64,1408]{2,1,0:T(8,128)(2,1)S(1)}, bf16[20,64,1408]{2,1,0:T(8,128)(2,1)}, u32[]{:S(2)}) %copy-start) | copy-done | bytes 3604504
  3.1 0.0 copy-start.1
  3.1 0.7 copy-done.1
  3.7 71.0 %shard_map.37 = f32[20,44,128]{2,1,0:T(8,128)S(1)} custom-call(s32[2]{0:T(128)S(1)} %copy-done.1, f32[322,128]{1,0:T(8,128)S(1)} %reshape.3.grid_ref, bf16[20,64,1408]{2,1,0:T(8,128)(2,1)S(1)} %copy-done), custom_call_target="tpu_custom_call" | custom-call | tf_op jit(solution)/shard_map/pallas_call | solution.py:438
  74.7 0.8 %copy.5 = f32[20,44,128]{2,1,0:T(8,128)} copy(f32[20,44,128]{2,1,0:T(8,128)S(1)} %shard_map.37) | data formatting | bytes 901120
Async XLA Ops:
  1.0 2.0 %copy-start = (bf16[20,64,1408]{2,1,0:T(8,128)(2,1)S(1)}, bf16[20,64,1408]{2,1,0:T(8,128)(2,1)}, u32[]{:S(2)}) copy-start(bf16[20,64,1408]{2,1,0:T(8,128)(2,1)} %leg_ref.1) | copy-start | bytes 10813444
  3.1 0.7 copy-start.1

commit v2 on v1

--- a/solution.py
+++ b/solution.py
@@ -39,10 +39,12 @@
 
 def kernel(
     sizes,
-    rows_ref,
-    grid_ref,
+    rows_hbm,
+    grid_hbm,
     leg_ref,
     out_ref,
+    rows_ref,
+    mine_raw,
     twin,
     folded,
     grid_high,
@@ -50,17 +52,20 @@
     window,
     leg_rows,
     weights,
-    send_r,
-    recv_r,
-    send_l,
-    recv_l,
+    sum_out,
+    sum_in,
+    term_out,
+    term_in,
     packed,
     blocks,
     spread,
     leg_sem,
+    own_sem,
     twin_sem,
-    ring_send,
-    ring_recv,
+    sum_send,
+    sum_recv,
+    term_send,
+    term_recv,
     y_send,
     y_recv,
     x_send,
@@ -69,6 +74,7 @@
     bands, sets, nx, pairs, slots, per_device = sizes
     ny, nz = bands // nx, sets // 2
     half = nz // 2
+    stages = half // 2
     trunc = 2 * pairs * sets - 1
     group_rows = 2 * pairs
     band, group = lax.axis_index("band"), lax.axis_index("set")
@@ -79,7 +85,6 @@
     def at_z(position):
         return lax.rem(position + nz, nz) * 2 + core
 
-    right, left = at_z(z + 1), at_z(z - 1)
 
     def at_y(position):
         return lax.rem(position + ny, ny) * nx + x
@@ -95,8 +100,8 @@
     def row_needs(side, of_y):
         return needs(side, of_y * nx + (0 if side == 0 else nx - 1))
 
-    peers = [(band, sibling), (band, right), (band, left)]
-    if nz == 2:
+    peers = [(band, sibling)] + [(band, at_z(z + d)) for d in (1, -1, 2, -2)]
+    if nz == 4:
         peers.pop()
     peers += [(at_y(y + d), group) for d in range(1, ny)]
     peers += [(at_x(x + d), group) for d in range(1, nx)]
@@ -110,13 +115,32 @@
         leg_ref.at[:, :, pl.ds(pl.multiple_of(start, 128), WINDOW)], window, leg_sem
     )
     leg_copy.start()
+    rows_copy = pltpu.make_async_copy(rows_hbm, rows_ref, own_sem.at[0])
+    rows_copy.start()
+    grid_copy = pltpu.make_async_copy(grid_hbm, mine_raw, own_sem.at[1])
+    grid_copy.start()
+    folded[:, per_device:, :] = jnp.zeros_like(folded[:, per_device:, :])
+    sum_in[0, 0, 0] = jnp.zeros_like(sum_in[0, 0, 0])
+    sum_in[1, 0, 1] = jnp.zeros_like(sum_in[1, 0, 1])
+    pl.semaphore_wait(barrier, len(peers))
+    swap = pltpu.make_async_remote_copy(
+        src_ref=grid_hbm,
+        dst_ref=twin,
+        send_sem=twin_sem.at[0],
+        recv_sem=twin_sem.at[1],
+        device_id=(band, sibling),
+        device_id_type=MESH,
+    )
+    swap.start()
+    rows_copy.wait()
+    grid_copy.wait()
 
     lengths = [rows_ref[q].astype(jnp.float32) for q in range(2)]
     bases = [group * per_device, sibling * per_device]
 
     def prepare(source, half_index):
         for q in range(2):
-            folded[q, 0:per_device, :] = source[pl.ds(q, per_device, stride=2), :]
+            folded[q, 0:per_device, :] = source[:, q, :]
         for q in range(2):
             value = folded[q]
             point = bases[half_index] + lax.broadcasted_iota(jnp.int32, value.shape, 0)
@@ -155,15 +179,25 @@
             results.append(total)
         return results
 
-    def ring_copy(to_right, slot, q):
+    def sum_copy(to_right, stage, q):
         side = 0 if to_right else 1
-        source, target = (send_r, recv_r) if to_right else (send_l, recv_l)
         return pltpu.make_async_remote_copy(
-            src_ref=source.at[slot, q],
-            dst_ref=target.at[slot, q],
-            send_sem=ring_send.at[side, slot, q],
-            recv_sem=ring_recv.at[side, slot, q],
-            device_id=(band, right if to_right else left),
+            src_ref=sum_out.at[side, stage, q],
+            dst_ref=sum_in.at[side, stage, q],
+            send_sem=sum_send.at[side, stage, q],
+            recv_sem=sum_recv.at[side, stage, q],
+            device_id=(band, at_z(z + 2 if to_right else z - 2)),
+            device_id_type=MESH,
+        )
+
+    def term_copy(to_right, stage):
+        side = 0 if to_right else 1
+        return pltpu.make_async_remote_copy(
+            src_ref=term_out.at[side, stage],
+            dst_ref=term_in.at[side, stage],
+            send_sem=term_send.at[side, stage],
+            recv_sem=term_recv.at[side, stage],
+            device_id=(band, at_z(z + 1 if to_right else z - 1)),
             device_id_type=MESH,
         )
 
@@ -183,33 +217,22 @@
         weights[0, pair] = jnp.where(is_first & even, turned, 0.0).astype(jnp.bfloat16)
         weights[1, pair] = jnp.where((~is_first) & other, turned, 0.0).astype(jnp.bfloat16)
 
-    folded[:, per_device:, :] = jnp.zeros_like(folded[:, per_device:, :])
-    recv_r[0, 0] = jnp.zeros_like(recv_r[0, 0])
-    recv_l[0, 1] = jnp.zeros_like(recv_l[0, 1])
-    prepare(grid_ref, 0)
-
-    pl.semaphore_wait(barrier, len(peers))
-    swap = pltpu.make_async_remote_copy(
-        src_ref=grid_ref,
-        dst_ref=twin,
-        send_sem=twin_sem.at[0],
-        recv_sem=twin_sem.at[1],
-        device_id=(band, sibling),
-        device_id_type=MESH,
-    )
-    swap.start()
+    prepare(mine_raw, 0)
     swap.wait()
     prepare(twin, 1)
 
     far = partials([at_z(z + half)])
-    send_l[0, 0] = far[0]
-    ring_copy(False, 0, 0).start()
-    send_r[0, 1] = far[1]
-    ring_copy(True, 0, 1).start()
-    leg_copy.wait()
-    per_step = -(-pairs // max(half - 1, 1))
+    sum_out[1, 0, 0] = far[0]
+    sum_copy(False, 0, 0).start()
+    sum_out[0, 0, 1] = far[1]
+    sum_copy(True, 0, 1).start()
+    per_step = -(-pairs // max(stages - 1, 1))
 
     def weights_step(step):
+        @pl.when(step == 1)
+        def _():
+            leg_copy.wait()
+
         def one(index, carry):
             pair = (step - 1) * per_step + index
 
@@ -221,40 +244,61 @@
 
         lax.fori_loop(0, per_step, one, 0)
 
-    def ring_step(step, carry):
-        mine = partials([at_z(z + half - step), at_z(z - half + step)])
+    def send_terms(stage):
+        distance = half - 2 * stage - 1
+        terms = partials([at_z(z + distance), at_z(z - distance)])
+        for side in range(2):
+            for q in range(2):
+                for part in range(2):
+                    low = (2 * part + side) * group_rows
+                    term_out[side, stage, q, part * group_rows : (part + 1) * group_rows] = terms[
+                        q
+                    ][low : low + group_rows].astype(term_out.dtype)
+            term_copy(side == 0, stage).start()
+
+    send_terms(0)
+
+    def stage_step(stage, carry):
+        send_terms(stage)
+        distance = half - 2 * stage
+        mine = partials([at_z(z + distance), at_z(z - distance)])
+        for side in range(2):
+            term_copy(side == 0, stage - 1).wait_recv()
         for q in range(2):
-            for to_right in (True, False):
-                source, came = (send_r, recv_r) if to_right else (send_l, recv_l)
-
-                @pl.when((step > 1) | (q == (1 if to_right else 0)))
+            for side in range(2):
+                @pl.when((stage > 1) | (q == 1 - side))
                 def _():
-                    ring_copy(to_right, step - 1, q).wait_recv()
-
-                offset = 0 if to_right else group_rows
+                    sum_copy(side == 0, stage - 1, q).wait_recv()
+
                 for part in range(2):
-                    low = 2 * part * group_rows + offset
+                    low = (2 * part + side) * group_rows
                     span = slice(part * group_rows, (part + 1) * group_rows)
-                    source[step, q, span] = (
-                        came[step - 1, q, span] + mine[q][low : low + group_rows]
+                    sum_out[side, stage, q, span] = (
+                        mine[q][low : low + group_rows]
+                        + term_in[side, stage - 1, q, span].astype(jnp.float32)
+                        + sum_in[side, stage - 1, q, span]
                     )
-                ring_copy(to_right, step, q).start()
-        weights_step(step)
-        return carry
-
-    lax.fori_loop(1, half, ring_step, 0)
-    if half == 1:
+                sum_copy(side == 0, stage, q).start()
+        weights_step(stage)
+        return carry
+
+    lax.fori_loop(1, stages, stage_step, 0)
+    if stages == 1:
         weights_step(1)
 
     own = partials([group])
-    last = half - 1
+    last = stages - 1
+    for side in range(2):
+        term_copy(side == 0, last).wait_recv()
     for q in range(2):
-        for to_right in (True, False):
-            if half > 1 or q == (1 if to_right else 0):
-                ring_copy(to_right, last, q).wait_recv()
+        for side in range(2):
+            if stages > 1 or q == 1 - side:
+                sum_copy(side == 0, last, q).wait_recv()
 
     for q in range(2):
-        total = own[q] + recv_r[last, q] + recv_l[last, q]
+        total = own[q]
+        for side in range(2):
+            total = total + sum_in[side, last, q] + term_in[side, last, q].astype(jnp.float32)
         index = lax.broadcasted_iota(jnp.int32, (group_rows, 128), 0)
         wave = jnp.where(index < pairs, pairs * group + index, trunc - pairs * group - (index - pairs))
         usable = wave <= lax.div(rows_ref[q] - 1, 2)
@@ -370,37 +414,49 @@
 
     lax.fori_loop(0, ny, collect, 0)
 
-    def legendre(side, add):
-        def one(pair, carry):
-            parts = [
-                spread[side, pl.ds((2 * parity + q) * pairs + pair, bands, stride=4 * pairs), :]
-                for parity in range(2)
-                for q in range(2)
-            ]
-            values = jnp.concatenate(parts, axis=0).astype(jnp.bfloat16)
-            result = jnp.dot(weights[side, pair], values, preferred_element_type=jnp.float32)
-            result = result[:slots]
-            out_ref[pair] = out_ref[pair] + result if add else result
+    def legendre(sides):
+        unroll = 4 if pairs % 4 == 0 else 1
+
+        def some(index, carry):
+            for step in range(unroll):
+                pair = index * unroll + step
+                total = None
+                for side in sides:
+                    parts = [
+                        spread[
+                            side, pl.ds((2 * parity + q) * pairs + pair, bands, stride=4 * pairs), :
+                        ]
+                        for parity in range(2)
+                        for q in range(2)
+                    ]
+                    values = jnp.concatenate(parts, axis=0).astype(jnp.bfloat16)
+                    result = jnp.dot(
+                        weights[side, pair], values, preferred_element_type=jnp.float32
+                    )[:slots]
+                    total = result if total is None else total + result
+                out_ref[pair] = total
             return carry
 
-        lax.fori_loop(0, pairs, one, 0)
-
-    pl.when(needs(0, band))(lambda: legendre(0, False))
-    pl.when(needs(1, band) & ~needs(0, band))(lambda: legendre(1, False))
-    pl.when(needs(1, band) & needs(0, band))(lambda: legendre(1, True))
-
-    for to_right in (True, False):
-        for q in range(2):
-            if q == (1 if to_right else 0):
-                ring_copy(to_right, 0, q).wait_send()
-
-    def ring_sent(step, carry):
-        for to_right in (True, False):
+        lax.fori_loop(0, pairs // unroll, some, 0)
+
+    pl.when(needs(0, band) & ~needs(1, band))(lambda: legendre((0,)))
+    pl.when(needs(1, band) & ~needs(0, band))(lambda: legendre((1,)))
+    pl.when(needs(1, band) & needs(0, band))(lambda: legendre((0, 1)))
+
+    sum_copy(False, 0, 0).wait_send()
+    sum_copy(True, 0, 1).wait_send()
+
+    def z_sent(stage, carry):
+        for side in range(2):
+            term_copy(side == 0, stage).wait_send()
             for q in range(2):
-                ring_copy(to_right, step, q).wait_send()
-        return carry
-
-    lax.fori_loop(1, half, ring_sent, 0)
+                @pl.when(stage > 0)
+                def _():
+                    sum_copy(side == 0, stage, q).wait_send()
+
+        return carry
+
+    lax.fori_loop(0, stages, z_sent, 0)
 
     def y_sent(distance, carry):
         for side in range(2):
@@ -429,47 +485,53 @@
     pairs, rows, width = legendre.shape
     slots = width // bands
     per_device = grid.shape[1]
-    points = jnp.transpose(grid, (1, 0, 2)).reshape(2 * per_device, 128)
-    half = sets // 4
+    points = jnp.transpose(grid, (1, 0, 2))
+    stages = sets // 8
     padded = -(-slots // 16) * 16
     group_rows = 2 * pairs
     f32, bf16 = jnp.float32, jnp.bfloat16
-    ring = pltpu.VMEM((half, 2, 2 * group_rows, 128), f32)
+    sums = pltpu.VMEM((2, stages, 2, 2 * group_rows, 128), f32)
+    terms = pltpu.VMEM((2, stages, 2, 2 * group_rows, 128), bf16)
     return pl.pallas_call(
         functools.partial(kernel, (bands, sets, nx, pairs, slots, per_device)),
         out_shape=jax.ShapeDtypeStruct((pairs, slots, 128), f32),
         in_specs=[
-            pl.BlockSpec(memory_space=pltpu.SMEM),
-            pl.BlockSpec(memory_space=pltpu.VMEM),
-            pl.BlockSpec(memory_space=pl.ANY),
+            pl.BlockSpec(memory_space=pltpu.HBM),
+            pl.BlockSpec(memory_space=pltpu.HBM),
+            pl.BlockSpec(memory_space=pltpu.HBM),
         ],
         out_specs=pl.BlockSpec(memory_space=pltpu.VMEM),
         scratch_shapes=[
-            pltpu.VMEM((2 * per_device, 128), f32),
+            pltpu.SMEM((2,), jnp.int32),
+            pltpu.VMEM((per_device, 2, 128), f32),
+            pltpu.VMEM((per_device, 2, 128), f32),
             pltpu.VMEM((2, 256, 128), f32),
             pltpu.VMEM((2, 2, 256, 128), bf16),
             pltpu.VMEM((2, 2, 256, 128), bf16),
             pltpu.VMEM((pairs, rows, WINDOW), bf16),
             pltpu.VMEM((rows, 128), f32),
             pltpu.VMEM((2, pairs, padded, 2 * rows), bf16),
-            ring,
-            ring,
-            ring,
-            ring,
+            sums,
+            sums,
+            terms,
+            terms,
             pltpu.VMEM((2, 4 * pairs, 128), f32),
             pltpu.VMEM((2, bands, 4 * pairs, 128), bf16),
             pltpu.VMEM((2, bands * 4 * pairs, 128), f32),
             pltpu.SemaphoreType.DMA,
             pltpu.SemaphoreType.DMA((2,)),
-            pltpu.SemaphoreType.DMA((2, half, 2)),
-            pltpu.SemaphoreType.DMA((2, half, 2)),
+            pltpu.SemaphoreType.DMA((2,)),
+            pltpu.SemaphoreType.DMA((2, stages, 2)),
+            pltpu.SemaphoreType.DMA((2, stages, 2)),
+            pltpu.SemaphoreType.DMA((2, stages)),
+            pltpu.SemaphoreType.DMA((2, stages)),
             pltpu.SemaphoreType.DMA((2, bands // nx)),
             pltpu.SemaphoreType.DMA((2, bands // nx)),
             pltpu.SemaphoreType.DMA((2, bands // nx, nx)),
             pltpu.SemaphoreType.DMA((2, bands)),
         ],
         compiler_params=pltpu.CompilerParams(
-            collective_id=0, has_side_effects=True, vmem_limit_bytes=40 * 1024 * 1024
+            collective_id=0, has_side_effects=True, vmem_limit_bytes=62900000
         ),
     )(row_points, points, legendre)
 

time: 75.7 us -> 66.3 us (0.88)
  Pallas kernels: 71 us -> 64.2 us
  local copies, waits for them, and re-layouts: 4.48 us -> 1.84 us
    pallas_call x1, Pallas kernels: 71 us -> 64.2 us  [shards(): pl.pallas_call(functools.partial(kernel, (bands, sets, nx, pairs, slots,...]
    unnamed x5 -> x1, local copies, waits for them, and re-layouts: 3.45 us -> 1.84 us
    reshape x1 -> x0, local copies, waits for them, and re-layouts: 1.03 us -> none  [shards(): points = jnp.transpose(grid, (1, 0, 2)).reshape(2 * per_device, 128)]
where the time goes in v2:
time: 66.3 us; the launch traced here: 66.1 us
  Pallas kernels  64.2 us (97%)
  local copies, waits for them, and re-layouts  1.84 us (3%)
    pallas_call x1, Pallas kernels, shards(): pl.pallas_call(functools.partial(kernel, (bands, sets, nx, pairs, slots,...  64.2 us
    unnamed x1, local copies, waits for them, and re-layouts  1.84 us

profile of v2, /device:TPU:56, one launch (start us, length us, event | category | flops | bytes accessed | tf_op | source)
XLA Modules:
  0.0 66.1 jit_solution(11527643587418672394)
XLA Ops:
  0.0 64.2 %shard_map.37 = f32[20,44,128]{2,1,0:T(8,128)} custom-call(s32[2]{0:T(128)} %rows_hbm.1, f32[161,2,128]{2,1,0:T(2,128)} %bitcast.1, bf16[20,64,1408]{2,1,0:T(8,128)(2,1)} %leg_ref.1), custom_call_target="tpu_custom_call" | custom-call | tf_op jit(solution)/shard_map/pallas_call | solution.py:495
  64.3 1.8 %copy.5 = f32[20,44,128]{2,1,0:T(8,128)} copy(f32[20,44,128]{2,1,0:T(8,128)} %shard_map.37) | data formatting | bytes 901120

commit v3 on v2

--- a/solution.py
+++ b/solution.py
@@ -52,6 +52,10 @@
     window,
     leg_rows,
     weights,
+    base_cos,
+    base_sin,
+    early_out,
+    early_in,
     sum_out,
     sum_in,
     term_out,
@@ -75,6 +79,7 @@
     ny, nz = bands // nx, sets // 2
     half = nz // 2
     stages = half // 2
+    early = early_in.shape[1]
     trunc = 2 * pairs * sets - 1
     group_rows = 2 * pairs
     band, group = lax.axis_index("band"), lax.axis_index("set")
@@ -120,9 +125,6 @@
     grid_copy = pltpu.make_async_copy(grid_hbm, mine_raw, own_sem.at[1])
     grid_copy.start()
     folded[:, per_device:, :] = jnp.zeros_like(folded[:, per_device:, :])
-    sum_in[0, 0, 0] = jnp.zeros_like(sum_in[0, 0, 0])
-    sum_in[1, 0, 1] = jnp.zeros_like(sum_in[1, 0, 1])
-    pl.semaphore_wait(barrier, len(peers))
     swap = pltpu.make_async_remote_copy(
         src_ref=grid_hbm,
         dst_ref=twin,
@@ -131,10 +133,7 @@
         device_id=(band, sibling),
         device_id_type=MESH,
     )
-    swap.start()
     rows_copy.wait()
-    grid_copy.wait()
-
     lengths = [rows_ref[q].astype(jnp.float32) for q in range(2)]
     bases = [group * per_device, sibling * per_device]
 
@@ -152,26 +151,40 @@
             value = jnp.where((point < rows_ref[q]) & (row < per_device), value, 0.0)
             grid_high[q, half_index], grid_low[q, half_index] = split(value)
 
+    def base_tables():
+        index = lax.broadcasted_iota(jnp.int32, (group_rows, 256), 0)
+        waves = jnp.where(index < pairs, index, trunc - (index - pairs)).astype(jnp.float32)
+        lane = lax.broadcasted_iota(jnp.int32, (group_rows, 256), 1)
+        for q in range(2):
+            length = jnp.full((group_rows, 256), lengths[q], jnp.float32)
+            for half_index in range(2):
+                points = (bases[half_index] + lane).astype(jnp.float32)
+                cosine, sine = cos_sin(waves, points, length)
+                base_cos[q, half_index] = cosine
+                base_sin[q, half_index] = sine
+
     def partials(owners):
         count = len(owners) * group_rows
-        index = lax.broadcasted_iota(jnp.int32, (count, 1), 0)
-        waves = jnp.zeros((count, 1), jnp.int32)
-        for position, owner in enumerate(owners):
-            inside = index - position * group_rows
-            here = jnp.where(
-                inside < pairs, pairs * owner + inside, trunc - pairs * owner - (inside - pairs)
-            )
-            waves = jnp.where(inside >= 0, here, waves)
-        waves = waves.astype(jnp.float32)
-        lane = lax.broadcasted_iota(jnp.int32, (1, 256), 1)
+        lane = lax.broadcasted_iota(jnp.int32, (8, 256), 1)
+        upward = lax.broadcasted_iota(jnp.int32, (group_rows, 256), 0) < pairs
         results = []
         for q in range(2):
-            length = jnp.full((1, 256), lengths[q], jnp.float32)
+            length = jnp.full((8, 256), lengths[q], jnp.float32)
             total = jnp.zeros((2 * count, 128), jnp.float32)
             for half_index in range(2):
                 points = (bases[half_index] + lane).astype(jnp.float32)
-                table = jnp.concatenate(cos_sin(waves, points, length), axis=0)
-                high, low = split(table)
+                cosine, sine = base_cos[q, half_index], base_sin[q, half_index]
+                cosines, sines = [], []
+                for owner in owners:
+                    waves = jnp.full((8, 256), pairs * owner, jnp.int32).astype(jnp.float32)
+                    turn_cos, turn_sin = (
+                        jnp.concatenate([part] * (group_rows // 8), axis=0)
+                        for part in cos_sin(waves, points, length)
+                    )
+                    turn_sin = jnp.where(upward, turn_sin, -turn_sin)
+                    cosines.append(cosine * turn_cos - sine * turn_sin)
+                    sines.append(sine * turn_cos + cosine * turn_sin)
+                high, low = split(jnp.concatenate(cosines + sines, axis=0))
                 for factor, values in ((high, grid_high), (low, grid_high), (high, grid_low)):
                     total = total + jnp.dot(
                         factor, values[q, half_index], preferred_element_type=jnp.float32
@@ -179,11 +192,15 @@
             results.append(total)
         return results
 
+    def sum_slots(stage):
+        return (early_out, early_in, stage) if stage < early else (sum_out, sum_in, stage - early)
+
     def sum_copy(to_right, stage, q):
         side = 0 if to_right else 1
+        source, target, slot = sum_slots(stage)
         return pltpu.make_async_remote_copy(
-            src_ref=sum_out.at[side, stage, q],
-            dst_ref=sum_in.at[side, stage, q],
+            src_ref=source.at[side, slot, q],
+            dst_ref=target.at[side, slot, q],
             send_sem=sum_send.at[side, stage, q],
             recv_sem=sum_recv.at[side, stage, q],
             device_id=(band, at_z(z + 2 if to_right else z - 2)),
@@ -217,20 +234,24 @@
         weights[0, pair] = jnp.where(is_first & even, turned, 0.0).astype(jnp.bfloat16)
         weights[1, pair] = jnp.where((~is_first) & other, turned, 0.0).astype(jnp.bfloat16)
 
+    base_tables()
+    pl.semaphore_wait(barrier, len(peers))
+    swap.start()
+    grid_copy.wait()
     prepare(mine_raw, 0)
     swap.wait()
     prepare(twin, 1)
 
     far = partials([at_z(z + half)])
-    sum_out[1, 0, 0] = far[0]
+    first_out = sum_slots(0)[0]
+    first_out[1, 0, 0] = far[0].astype(first_out.dtype)
     sum_copy(False, 0, 0).start()
-    sum_out[0, 0, 1] = far[1]
+    first_out[0, 0, 1] = far[1].astype(first_out.dtype)
     sum_copy(True, 0, 1).start()
     per_step = -(-pairs // max(stages - 1, 1))
 
     def weights_step(step):
-        @pl.when(step == 1)
-        def _():
+        if step == 1:
             leg_copy.wait()
 
         def one(index, carry):
@@ -258,31 +279,29 @@
 
     send_terms(0)
 
-    def stage_step(stage, carry):
+    for stage in range(1, stages):
         send_terms(stage)
         distance = half - 2 * stage
         mine = partials([at_z(z + distance), at_z(z - distance)])
         for side in range(2):
             term_copy(side == 0, stage - 1).wait_recv()
+        source, _, slot = sum_slots(stage)
+        _, came, came_slot = sum_slots(stage - 1)
         for q in range(2):
             for side in range(2):
-                @pl.when((stage > 1) | (q == 1 - side))
-                def _():
+                has_sum = stage > 1 or q == 1 - side
+                if has_sum:
                     sum_copy(side == 0, stage - 1, q).wait_recv()
-
                 for part in range(2):
                     low = (2 * part + side) * group_rows
                     span = slice(part * group_rows, (part + 1) * group_rows)
-                    sum_out[side, stage, q, span] = (
-                        mine[q][low : low + group_rows]
-                        + term_in[side, stage - 1, q, span].astype(jnp.float32)
-                        + sum_in[side, stage - 1, q, span]
-                    )
+                    total = mine[q][low : low + group_rows]
+                    total = total + term_in[side, stage - 1, q, span].astype(jnp.float32)
+                    if has_sum:
+                        total = total + came[side, came_slot, q, span].astype(jnp.float32)
+                    source[side, slot, q, span] = total.astype(source.dtype)
                 sum_copy(side == 0, stage, q).start()
         weights_step(stage)
-        return carry
-
-    lax.fori_loop(1, stages, stage_step, 0)
     if stages == 1:
         weights_step(1)
 
@@ -297,8 +316,11 @@
 
     for q in range(2):
         total = own[q]
-        for side in range(2):
-            total = total + sum_in[side, last, q] + term_in[side, last, q].astype(jnp.float32)
+        _, came, slot = sum_slots(last)
+        for side in range(2):
+            total = total + term_in[side, last, q].astype(jnp.float32)
+            if stages > 1 or q == 1 - side:
+                total = total + came[side, slot, q].astype(jnp.float32)
         index = lax.broadcasted_iota(jnp.int32, (group_rows, 128), 0)
         wave = jnp.where(index < pairs, pairs * group + index, trunc - pairs * group - (index - pairs))
         usable = wave <= lax.div(rows_ref[q] - 1, 2)
@@ -446,17 +468,12 @@
     sum_copy(False, 0, 0).wait_send()
     sum_copy(True, 0, 1).wait_send()
 
-    def z_sent(stage, carry):
+    for stage in range(stages):
         for side in range(2):
             term_copy(side == 0, stage).wait_send()
             for q in range(2):
-                @pl.when(stage > 0)
-                def _():
+                if stage:
                     sum_copy(side == 0, stage, q).wait_send()
-
-        return carry
-
-    lax.fori_loop(0, stages, z_sent, 0)
 
     def y_sent(distance, carry):
         for side in range(2):
@@ -490,7 +507,10 @@
     padded = -(-slots // 16) * 16
     group_rows = 2 * pairs
     f32, bf16 = jnp.float32, jnp.bfloat16
-    sums = pltpu.VMEM((2, stages, 2, 2 * group_rows, 128), f32)
+    table = pltpu.VMEM((2, 2, group_rows, 256), f32)
+    early = min(2, stages)
+    early_sums = pltpu.VMEM((2, early, 2, 2 * group_rows, 128), bf16)
+    sums = pltpu.VMEM((2, max(stages - early, 1), 2, 2 * group_rows, 128), f32)
     terms = pltpu.VMEM((2, stages, 2, 2 * group_rows, 128), bf16)
     return pl.pallas_call(
         functools.partial(kernel, (bands, sets, nx, pairs, slots, per_device)),
@@ -511,6 +531,10 @@
             pltpu.VMEM((pairs, rows, WINDOW), bf16),
             pltpu.VMEM((rows, 128), f32),
             pltpu.VMEM((2, pairs, padded, 2 * rows), bf16),
+            table,
+            table,
+            early_sums,
+            early_sums,
             sums,
             sums,
             terms,

time: 66.3 us -> 63.2 us (0.953)
  Pallas kernels: 64.2 us -> 61.1 us
    pallas_call x1, Pallas kernels: 64.2 us -> 61.1 us  [shards(): pl.pallas_call(functools.partial(kernel, (bands, sets, nx, pairs, slots,...]
where the time goes in v3:
time: 63.2 us; the launch traced here: 63 us
  Pallas kernels  61.1 us (97%)
  local copies, waits for them, and re-layouts  1.84 us (3%)
    pallas_call x1, Pallas kernels, shards(): pl.pallas_call(functools.partial(kernel, (bands, sets, nx, pairs, slots,...  61.1 us
    unnamed x1, local copies, waits for them, and re-layouts  1.84 us

profile of v3, /device:TPU:56, one launch (start us, length us, event | category | flops | bytes accessed | tf_op | source)
XLA Modules:
  0.0 63.0 jit_solution(5054865322375173331)
XLA Ops:
  0.0 61.1 %shard_map.37 = f32[20,44,128]{2,1,0:T(8,128)} custom-call(s32[2]{0:T(128)} %rows_hbm.1, f32[161,2,128]{2,1,0:T(2,128)} %bitcast.1, bf16[20,64,1408]{2,1,0:T(8,128)(2,1)} %leg_ref.1), custom_call_target="tpu_custom_call" | custom-call | tf_op jit(solution)/shard_map/pallas_call | solution.py:515
  61.1 1.8 %copy.5 = f32[20,44,128]{2,1,0:T(8,128)} copy(f32[20,44,128]{2,1,0:T(8,128)} %shard_map.37) | data formatting | bytes 901120

commit v4 on v3

--- a/solution.py
+++ b/solution.py
@@ -105,6 +105,12 @@
     def row_needs(side, of_y):
         return needs(side, of_y * nx + (0 if side == 0 else nx - 1))
 
+    stride = (trunc + 1) // (2 * bands)
+
+    def holds(side, of_band):
+        lowest = pairs * group if side == 0 else trunc - pairs * group - (pairs - 1)
+        return lowest <= 4 * stride * (of_band + 1) + 7
+
     peers = [(band, sibling)] + [(band, at_z(z + d)) for d in (1, -1, 2, -2)]
     if nz == 4:
         peers.pop()
@@ -253,6 +259,7 @@
     def weights_step(step):
         if step == 1:
             leg_copy.wait()
+            spread[...] = jnp.zeros_like(spread)
 
         def one(index, carry):
             pair = (step - 1) * per_step + index
@@ -388,7 +395,7 @@
     def y_start(index, carry):
         distance = lax.rem(in_turn(index), ny)
         for side in range(2):
-            @pl.when(row_needs(side, lax.rem(y + distance, ny)))
+            @pl.when(row_needs(side, lax.rem(y + distance, ny)) & holds(side, band))
             def _():
                 y_copy(side, distance).start()
 
@@ -405,16 +412,18 @@
     def forward(index, carry):
         source_y = lax.rem(y + in_turn(index), ny)
         for side in range(2):
-            @pl.when(row_needs(side, y) & (index > 0))
+            held = holds(side, source_y * nx + x)
+
+            @pl.when(row_needs(side, y) & (index > 0) & held)
             def _():
                 y_arrival(side, source_y).wait_recv()
 
             for distance in range(1, nx):
-                @pl.when(needs(side, at_x(x + distance)))
+                @pl.when(needs(side, at_x(x + distance)) & held)
                 def _():
                     x_copy(side, source_y, distance).start()
 
-            @pl.when(needs(side, band))
+            @pl.when(needs(side, band) & held)
             def _():
                 unpack(side, source_y * nx + x)
 
@@ -426,9 +435,10 @@
         source_y = lax.rem(y + in_turn(index), ny)
         for side in range(2):
             for distance in range(1, nx):
-                @pl.when(needs(side, band))
+                source = source_y * nx + lax.rem(x + distance, nx)
+
+                @pl.when(needs(side, band) & holds(side, source))
                 def _():
-                    source = source_y * nx + lax.rem(x + distance, nx)
                     x_arrival(side, source).wait_recv()
                     unpack(side, source)
 
@@ -477,7 +487,7 @@
 
     def y_sent(distance, carry):
         for side in range(2):
-            @pl.when(row_needs(side, lax.rem(y + distance, ny)))
+            @pl.when(row_needs(side, lax.rem(y + distance, ny)) & holds(side, band))
             def _():
                 y_copy(side, distance).wait_send()
 
@@ -488,7 +498,7 @@
     def x_sent(source_y, carry):
         for side in range(2):
             for distance in range(1, nx):
-                @pl.when(needs(side, at_x(x + distance)))
+                @pl.when(needs(side, at_x(x + distance)) & holds(side, source_y * nx + x))
                 def _():
                     x_copy(side, source_y, distance).wait_send()
 

time: 63.2 us -> 60 us (0.949)
  Pallas kernels: 61.1 us -> 58 us
    pallas_call x1, Pallas kernels: 61.1 us -> 58 us  [shards(): pl.pallas_call(functools.partial(kernel, (bands, sets, nx, pairs, slots,...]
where the time goes in v4:
time: 60 us; the launch traced here: 59.8 us
  Pallas kernels  58 us (97%)
  local copies, waits for them, and re-layouts  1.84 us (3%)
    pallas_call x1, Pallas kernels, shards(): pl.pallas_call(functools.partial(kernel, (bands, sets, nx, pairs, slots,...  58 us
    unnamed x1, local copies, waits for them, and re-layouts  1.84 us

profile of v4, /device:TPU:56, one launch (start us, length us, event | category | flops | bytes accessed | tf_op | source)
XLA Modules:
  0.0 59.8 jit_solution(5887961477971124799)
XLA Ops:
  0.0 58.0 %shard_map.37 = f32[20,44,128]{2,1,0:T(8,128)} custom-call(s32[2]{0:T(128)} %rows_hbm.1, f32[161,2,128]{2,1,0:T(2,128)} %bitcast.1, bf16[20,64,1408]{2,1,0:T(8,128)(2,1)} %leg_ref.1), custom_call_target="tpu_custom_call" | custom-call | tf_op jit(solution)/shard_map/pallas_call | solution.py:525
  58.0 1.8 %copy.5 = f32[20,44,128]{2,1,0:T(8,128)} copy(f32[20,44,128]{2,1,0:T(8,128)} %shard_map.37) | data formatting | bytes 901120

commit v5 on v4

--- a/solution.py
+++ b/solution.py
@@ -128,12 +128,14 @@
     leg_copy.start()
     rows_copy = pltpu.make_async_copy(rows_hbm, rows_ref, own_sem.at[0])
     rows_copy.start()
-    grid_copy = pltpu.make_async_copy(grid_hbm, mine_raw, own_sem.at[1])
+    grid_copy = pltpu.make_async_copy(
+        grid_hbm, mine_raw.at[pl.ds(0, per_device)], own_sem.at[1]
+    )
     grid_copy.start()
     folded[:, per_device:, :] = jnp.zeros_like(folded[:, per_device:, :])
     swap = pltpu.make_async_remote_copy(
         src_ref=grid_hbm,
-        dst_ref=twin,
+        dst_ref=twin.at[pl.ds(0, per_device)],
         send_sem=twin_sem.at[0],
         recv_sem=twin_sem.at[1],
         device_id=(band, sibling),
@@ -145,7 +147,7 @@
 
     def prepare(source, half_index):
         for q in range(2):
-            folded[q, 0:per_device, :] = source[:, q, :]
+            folded[q, 0:per_device, :] = source[0:per_device, q, :]
         for q in range(2):
             value = folded[q]
             point = bases[half_index] + lax.broadcasted_iota(jnp.int32, value.shape, 0)
@@ -227,7 +229,7 @@
     def weights_of(pair):
         values = window[pair].astype(jnp.float32)
         values = pltpu.roll(values, lax.rem(WINDOW - (first - start), WINDOW), 1)[:, :128]
-        leg_rows[...] = values
+        leg_rows[0 : values.shape[0], :] = values
         rows = jnp.concatenate([leg_rows[pl.ds(q, bands, stride=2), :] for q in range(2)], axis=0)
         turned = jnp.transpose(rows)[: weights.shape[2]]
         turned = jnp.concatenate([turned, turned], axis=1)
@@ -343,7 +345,7 @@
                 at = (parity * 2 + q) * pairs
                 packed[side, at : at + pairs] = parts[parity][side * pairs : (side + 1) * pairs]
     for side in range(2):
-        blocks[side, band] = packed[side].astype(jnp.bfloat16)
+        blocks[side, band] = packed[side, 0 : 4 * pairs].astype(jnp.bfloat16)
 
     def y_copy(side, distance):
         return pltpu.make_async_remote_copy(
@@ -533,13 +535,13 @@
         out_specs=pl.BlockSpec(memory_space=pltpu.VMEM),
         scratch_shapes=[
             pltpu.SMEM((2,), jnp.int32),
-            pltpu.VMEM((per_device, 2, 128), f32),
-            pltpu.VMEM((per_device, 2, 128), f32),
+            pltpu.VMEM((-(-per_device // 8) * 8, 2, 128), f32),
+            pltpu.VMEM((-(-per_device // 8) * 8, 2, 128), f32),
             pltpu.VMEM((2, 256, 128), f32),
             pltpu.VMEM((2, 2, 256, 128), bf16),
             pltpu.VMEM((2, 2, 256, 128), bf16),
             pltpu.VMEM((pairs, rows, WINDOW), bf16),
-            pltpu.VMEM((rows, 128), f32),
+            pltpu.VMEM((rows + 8, 128), f32),
             pltpu.VMEM((2, pairs, padded, 2 * rows), bf16),
             table,
             table,
@@ -549,9 +551,9 @@
             sums,
             terms,
             terms,
-            pltpu.VMEM((2, 4 * pairs, 128), f32),
+            pltpu.VMEM((2, 4 * pairs + 8, 128), f32),
             pltpu.VMEM((2, bands, 4 * pairs, 128), bf16),
-            pltpu.VMEM((2, bands * 4 * pairs, 128), f32),
+            pltpu.VMEM((2, (bands + 1) * 4 * pairs, 128), f32),
             pltpu.SemaphoreType.DMA,
             pltpu.SemaphoreType.DMA((2,)),
             pltpu.SemaphoreType.DMA((2,)),

time: 60 us -> 60.1 us (level)
  no operation moved by 1% of the time
where the time goes in v5:
time: 60.1 us; the launch traced here: 59.9 us
  Pallas kernels  58 us (97%)
  local copies, waits for them, and re-layouts  1.84 us (3%)
    pallas_call x1, Pallas kernels, shards(): pl.pallas_call(functools.partial(kernel, (bands, sets, nx, pairs, slots,...  58 us
    unnamed x1, local copies, waits for them, and re-layouts  1.84 us

profile of v5, /device:TPU:56, one launch (start us, length us, event | category | flops | bytes accessed | tf_op | source)
XLA Modules:
  0.0 59.9 jit_solution(17225379652915374760)
XLA Ops:
  0.0 58.0 %shard_map.37 = f32[20,44,128]{2,1,0:T(8,128)} custom-call(s32[2]{0:T(128)} %rows_hbm.1, f32[161,2,128]{2,1,0:T(2,128)} %bitcast.1, bf16[20,64,1408]{2,1,0:T(8,128)(2,1)} %leg_ref.1), custom_call_target="tpu_custom_call" | custom-call | tf_op jit(solution)/shard_map/pallas_call | solution.py:527
  58.0 1.8 %copy.5 = f32[20,44,128]{2,1,0:T(8,128)} copy(f32[20,44,128]{2,1,0:T(8,128)} %shard_map.37) | data formatting | bytes 901120
